TPU v7x, 512 devices: a whole 4x8x8 slice. The times are simulated.
512 devices in a mesh: replica: 64 (over x, y, core), tensor: 8 (over z).
Axes of the slice: x: 4, y: 8, z: 8, core: 2. Of those that a mesh axis runs over, the one named last changes fastest.
Arguments:
- features: bfloat16 [4096, 4, 7680], P('replica', None, 'tensor'), may hold values from -6 to 6
- kv_weight: bfloat16 [7680, 8, 256], P('tensor'), may hold values from -0.0625 to 0.0625
- image_owner: int32 [4096], replicated, may hold values from 0 to 63, as said below
- image_request: int32 [4096], replicated, may hold values from 0 to 7, as said below
- cross_query: bfloat16 [512, 64, 128], P('replica', 'tensor'), may hold values from -6 to 6
- self_query: bfloat16 [512, 64, 128], P('replica', 'tensor'), may hold values from -2.5 to 2.5
- self_cache: bfloat16 [512, 128, 8, 256], P('replica', None, 'tensor'), may hold values from -2.5 to 2.5
- fresh_key_value: bfloat16 [512, 8, 256], P('replica', 'tensor'), may hold values from -2.5 to 2.5
- cache_len: int32 [512], P('replica'), may hold values from 1 to 128, 32768 in all
Outputs:
- cross_out: bfloat16 [512, 64, 128], P('replica', 'tensor')
- self_out: bfloat16 [512, 64, 128], P('replica', 'tensor')
Inputs may be any that keep to these rules, and one draw needn't show every extreme that they name: `image_owner`: within each aligned block of 64 consecutive images (the images of one replica group), no decode replica owns more than 2 images, and one decode replica owns exactly 2 images in every block. `image_request`: some requests have no image.
All inputs are finite; a program needn't handle non-finite values. No bound on the sum of `cache_len` on one device may be relied on, other than what follows from the above.
Results may differ from a plain program's by a relative error of at most 0.02.
Values may be sent and summed in bfloat16 or wider, within the bound.
No kernel may reach another device: no remote copies, remote signals or barrier semaphores. Data moves between devices by JAX's collectives and lax.ppermute only.
A program may use at most 64 MiB of HBM per device.

v0:
```python
import math

import jax
import jax.numpy as jnp
from jax import lax
from jax.sharding import PartitionSpec as P


def local(
    features,
    kv_weight,
    image_owner,
    image_request,
    cross_query,
    self_query,
    self_cache,
    fresh_key_value,
    cache_len,
):
    n_rep = lax.axis_size("replica")
    me_rep = lax.axis_index("replica")
    images, patches, block = features.shape
    kvh_all = kv_weight.shape[1]
    width2 = kv_weight.shape[2]
    head_width = width2 // 2
    score_scale = 1.0 / math.sqrt(head_width)
    slot_cap = max(2, 2 * images // n_rep)
    slot_all = n_rep * slot_cap
    owners = image_owner.reshape(n_rep, images)
    requests = image_request.reshape(n_rep, images)
    own_block = lax.dynamic_index_in_dim(owners, me_rep, 0, keepdims=False)
    positions = jnp.arange(images, dtype=jnp.int32)
    same_owner = own_block[:, None] == own_block[None, :]
    earlier = positions[:, None] > positions[None, :]
    rank = jnp.sum((same_owner & earlier).astype(jnp.int32), axis=1, dtype=jnp.int32)
    slot = own_block * slot_cap + rank
    placing = (jnp.arange(slot_all, dtype=jnp.int32)[:, None] == slot[None, :]).astype(jnp.bfloat16)
    weight_flat = kv_weight.reshape(block, kvh_all * width2)
    sq_heads = self_query.shape[1]
    kvh_local = self_cache.shape[2]
    group = sq_heads // kvh_local
    req_count = self_query.shape[0]
    self_query_rows = self_query.reshape(req_count, kvh_local, group, head_width)
    scores = (
        jnp.einsum(
            "bkgd,bskd->bkgs",
            self_query_rows,
            self_cache[..., :head_width],
            preferred_element_type=jnp.float32,
        )
        * score_scale
    )
    live = jnp.arange(self_cache.shape[1], dtype=jnp.int32)[None, :] < cache_len[:, None]
    weight = jnp.where(live[:, None, None, :], jnp.exp(scores), jnp.float32(0.0))
    fresh_weight = jnp.exp(
        jnp.einsum(
            "ptwe,pte->ptw",
            self_query_rows,
            fresh_key_value[..., :head_width],
            preferred_element_type=jnp.float32,
        )
        * score_scale
    )
    total = jnp.sum(weight, axis=-1) + fresh_weight
    numer = jnp.einsum(
        "bkgs,bskd->bkgd",
        weight.astype(jnp.bfloat16),
        self_cache[..., head_width:],
        preferred_element_type=jnp.float32,
    )
    numer = numer + fresh_weight.astype(jnp.bfloat16).astype(jnp.float32)[
        ..., None
    ] * fresh_key_value[:, :, None, head_width:].astype(jnp.float32)
    self_out = (
        (numer / total[..., None]).astype(jnp.bfloat16).reshape(req_count, sq_heads, head_width)
    )
    outgoing = jnp.dot(
        placing, features.reshape(images, patches * block), preferred_element_type=jnp.float32
    )
    outgoing = outgoing.astype(jnp.bfloat16).reshape(n_rep, slot_cap, patches * block)
    arrived = lax.all_to_all(outgoing, "replica", split_axis=0, concat_axis=0, tiled=True)
    count = arrived.shape[1]
    flat = arrived.reshape(n_rep * count * patches, block)
    product = jnp.dot(flat, weight_flat, preferred_element_type=jnp.float32)
    partial_value = product.reshape(n_rep, count, patches, kvh_all, width2)
    summed = lax.psum_scatter(
        partial_value.astype(jnp.bfloat16), "tensor", scatter_dimension=3, tiled=True
    )
    image_kv = summed.reshape(slot_all * patches, kvh_local, width2)
    owner_match = (owners == me_rep).astype(jnp.int32)
    rank_all = jnp.cumsum(owner_match, axis=1, dtype=jnp.int32) - owner_match
    slot_ids = jnp.arange(slot_cap, dtype=jnp.int32)
    chosen = owner_match[:, None, :] * (rank_all[:, None, :] == slot_ids[None, :, None]).astype(
        jnp.int32
    )
    slot_live = jnp.sum(chosen, axis=-1, dtype=jnp.int32)
    slot_req = jnp.sum(chosen * requests[:, None, :], axis=-1, dtype=jnp.int32)
    row_live = (
        jnp.broadcast_to(slot_live[:, :, None], (n_rep, slot_cap, patches)).reshape(
            slot_all * patches
        )
        > 0
    )
    row_req = jnp.broadcast_to(slot_req[:, :, None], (n_rep, slot_cap, patches)).reshape(
        slot_all * patches
    )
    unscaled_keys = image_kv[..., :head_width].astype(jnp.float32)
    image_keys = (
        unscaled_keys
        * lax.rsqrt(jnp.mean(unscaled_keys * unscaled_keys, axis=-1, keepdims=True) + 1e-05)
    ).astype(jnp.bfloat16)
    image_values = image_kv[..., head_width:]
    cquery = cross_query.reshape(req_count, kvh_local, group, head_width)
    cscores = (
        jnp.einsum("bkgd,skd->bkgs", cquery, image_keys, preferred_element_type=jnp.float32)
        * score_scale
    )
    mask = row_live[None, :] & (row_req[None, :] == jnp.arange(req_count, dtype=jnp.int32)[:, None])
    cweight = jnp.where(mask[:, None, None, :], jnp.exp(cscores), jnp.float32(0.0))
    ctotal = jnp.sum(cweight, axis=-1)
    cnumer = jnp.einsum(
        "bkgs,skd->bkgd",
        cweight.astype(jnp.bfloat16),
        image_values,
        preferred_element_type=jnp.float32,
    )
    has_image = jnp.any(mask, axis=1)
    safe = jnp.where(has_image[:, None, None], ctotal, jnp.float32(1.0))
    cross_out = jnp.where(
        has_image[:, None, None, None], cnumer / safe[..., None], jnp.float32(0.0)
    )
    cross_out = cross_out.astype(jnp.bfloat16).reshape(req_count, sq_heads, head_width)
    return (cross_out, self_out)


def solution(mesh):
    return jax.shard_map(
        local,
        mesh=mesh,
        in_specs=(
            P("replica", None, "tensor"),
            P("tensor", None, None),
            P(),
            P(),
            P("replica", "tensor", None),
            P("replica", "tensor", None),
            P("replica", None, "tensor", None),
            P("replica", "tensor", None),
            P("replica"),
        ),
        out_specs=(P("replica", "tensor", None), P("replica", "tensor", None)),
        check_vma=False,
    )
```

profile of v0, /device:TPU:6, one launch (start us, length us, event | category | flops | bytes accessed | tf_op | source)
XLA Modules:
  0.0 155.7 jit_solution(1090064264738558511)
XLA Ops:
  7.2 0.8 reshape.229
  8.0 0.2 convert_reduce_fusion
  8.2 1.7 %reshape.230 = bf16[64,3840]{1,0:T(8,128)(2,1)S(1)} reshape(bf16[64,4,960]{2,1,0:T(4,128)(2,1)} %param.9) | data formatting | bytes 983040 | tf_op jit(solution)/shard_map/reshape | solution.py:78
  9.9 0.4 convolution_convert_fusion
  10.3 1.3 reshape.231
  11.6 10.8 %all-to-all-start = ((bf16[64,2,3840]{2,1,0:T(2,128)(2,1)}), bf16[64,2,3840]{2,1,0:T(2,128)(2,1)S(1)}, u32[]{:S(2)}, u32[]{:S(2)}) async-start(bf16[64,2,3840]{2,1,0:T(2,128)(2,1)} %reshape.231), calls=%async_computation | async-start | bytes 1966080 | tf_op jit(solution)/shard_map/all_to_all | solution.py:81
  22.5 0.2 reduce_window_sum.11
  22.8 25.0 %all-to-all-done = bf16[64,2,3840]{2,1,0:T(2,128)(2,1)S(1)} async-done(((bf16[64,2,3840]{2,1,0:T(2,128)(2,1)}), bf16[64,2,3840]{2,1,0:T(2,128)(2,1)S(1)}, u32[]{:S(2)}, u32[]{:S(2)}) %all-to-all-start) | async-done | bytes 983072 | tf_op jit(solution)/shard_map/all_to_all | solution.py:81
  47.8 1.2 reshape.248
  49.1 6.1 %fusion.2 = bf16[64,2,4,8,256]{4,0,3,2,1:T(8,128)(2,1)} fusion(bf16[8,256,960,1,1]{1,0,2,4,3:T(8,128)(2,1)} %bitcast.89, bf16[64,2,4,960,1]{3,2,1,0,4:T(4,128)(2,1)S(1)} %bitcast.87), kind=kOutput, calls=%fused_computation.3 | convolution fusion | flops 2014314496 | bytes 7012352 | tf_op jit(solution)/shard_map/dot_general | solution.py:84
  55.3 0.1 select_reduce_fusion
  55.5 0.1 broadcast_in_dim.45
  55.7 0.1 eq.84
  55.9 0.1 broadcast_in_dim.44
  56.2 1.3 dynamic-slice
  57.7 0.1 fusion.30
  57.8 0.3 fusion.39
  58.1 0.8 fusion.14
  58.9 86.7 %all-reduce.3.cloned.1.call-done = bf16[64,2,4,8,256]{4,0,3,2,1:T(8,128)(2,1)} async-done(((bf16[64,2,4,8,256]{4,0,3,2,1:T(8,128)(2,1)}), bf16[64,2,4,8,256]{4,0,3,2,1:T(8,128)(2,1)}) %all-reduce.3.cloned.1.call-update) | async-done | bytes 2097168
  145.6 1.6 %constant_dynamic-slice_fusion = bf16[64,2,4,1,256]{4,0,3,2,1:T(8,128)(2,1)S(1)} fusion(bf16[64,2,4,8,256]{4,0,3,2,1:T(8,128)(2,1)} %all-reduce.3.cloned.1.call-done, u32[]{:T(128)} %bitcast.33), kind=kLoop, calls=%fused_computation.56 | loop fusion | bytes 524292
  147.2 0.2 copy.30
  147.5 0.1 fusion.17
  147.7 0.4 fusion.38
  148.1 0.8 fusion.15
  (30 shorter events, 0.9 us)
Async XLA Ops:
  7.2 140.5 %copy-start = (bf16[8,8,128]{2,1,0:T(8,128)(2,1)S(1)}, bf16[8,8,128]{2,1,0:T(8,128)(2,1)}, u32[]{:S(2)}) copy-start(bf16[8,8,128]{2,1,0:T(8,128)(2,1)} %param.13) | copy-start | bytes 49156
  7.2 15.6 %copy-start.1 = (s32[4096]{0:T(1024)S(1)}, s32[4096]{0:T(1024)}, u32[]{:S(2)}) copy-start(s32[4096]{0:T(1024)} %param.12) | copy-start | bytes 49156
  11.6 36.2 %all-to-all-start = ((bf16[64,2,3840]{2,1,0:T(2,128)(2,1)}), bf16[64,2,3840]{2,1,0:T(2,128)(2,1)S(1)}, u32[]{:S(2)}, u32[]{:S(2)}) async-start(bf16[64,2,3840]{2,1,0:T(2,128)(2,1)} %reshape.231), calls=%async_computation | async-start | bytes 1966080 | tf_op jit(solution)/shard_map/all_to_all | solution.py:81
  22.4 123.2 %all-reduce.3.cloned.1.call-start = ((), (), s32[]{:S(2)}) async-start(), calls=%async_computation.1 | async-start | bytes 4194304
  49.0 8.4 %copy-start.5 = (s32[8]{0:T(128)S(1)}, s32[8]{0:T(128)}, u32[]{:S(2)}) copy-start(s32[8]{0:T(128)} %param.17) | copy-start | bytes 100
  49.0 8.5 %copy-start.2 = (bf16[8,1,256]{2,0,1:T(8,128)(2,1)S(1)}, bf16[8,1,256]{2,0,1:T(8,128)(2,1)}, u32[]{:S(2)}) copy-start(bf16[8,1,256]{2,0,1:T(8,128)(2,1)} %param.16) | copy-start | bytes 12292
  49.1 8.6 %copy-start.4 = (bf16[8,8,128]{2,1,0:T(8,128)(2,1)S(1)}, bf16[8,8,128]{2,1,0:T(8,128)(2,1)}, u32[]{:S(2)}) copy-start(bf16[8,8,128]{2,1,0:T(8,128)(2,1)} %param.14) | copy-start | bytes 49156
  49.1 8.7 %copy-start.3 = (bf16[8,128,1,256]{3,1,2,0:T(8,128)(2,1)S(1)}, bf16[8,128,1,256]{3,1,2,0:T(8,128)(2,1)}, u32[]{:S(2)}) copy-start(bf16[8,128,1,256]{3,1,2,0:T(8,128)(2,1)} %param.15) | copy-start | bytes 1572868
Sparse Core Ops, SparseCore 0:
  55.4 90.1 all-reduce.2
where the time goes:
time: 156 us
  waiting for transfers between devices  112 us (72%)
  between operations  14.2 us (9%)
  starting transfers between devices  10.8 us (7%)
  local copies, waits for them, and re-layouts  9.05 us (6%)
  matrix products  8.93 us (6%)
    unnamed x2, waiting for transfers between devices  86.7 us
    all_to_all x1, waiting for transfers between devices, local(): lax.all_to_all(outgoing, 'replica', split_axis=0, concat_axis=0, tiled=True)  25 us
    all_to_all x1, starting transfers between devices, local(): lax.all_to_all(outgoing, 'replica', split_axis=0, concat_axis=0, tiled=True)  10.8 us
    dot_general x1, matrix products, local(): product = jnp.dot(flat, weight_flat, preferred_element_type=jnp.float32)  6.15 us
  transfers between devices with their start and end apart: 2, of which 2 were waited for; matrix products, arithmetic and copies ran while one was open for 3% of the time, Pallas kernels for 0%

commit v1 on v0

--- a/solution.py
+++ b/solution.py
@@ -18,14 +18,28 @@
     cache_len,
 ):
     n_rep = lax.axis_size("replica")
+    n_ten = lax.axis_size("tensor")
     me_rep = lax.axis_index("replica")
     images, patches, block = features.shape
-    kvh_all = kv_weight.shape[1]
-    width2 = kv_weight.shape[2]
+    kvh_all, width2 = kv_weight.shape[1:]
     head_width = width2 // 2
     score_scale = 1.0 / math.sqrt(head_width)
     slot_cap = max(2, 2 * images // n_rep)
     slot_all = n_rep * slot_cap
+    rows = images * patches
+    req_count, sq_heads, _ = self_query.shape
+    kvh_local = self_cache.shape[2]
+    group = sq_heads // kvh_local
+
+    flat = features.reshape(rows, block)
+    partial = lax.dot_general(
+        flat, kv_weight, (((1,), (0,)), ((), ())), preferred_element_type=jnp.float32
+    ).astype(jnp.bfloat16)
+    partial = jnp.transpose(partial, (1, 0, 2))
+    shares = lax.all_to_all(partial, "tensor", split_axis=0, concat_axis=0, tiled=True)
+    shares = shares.reshape(n_ten, kvh_local * rows, width2)
+    image_kv = jnp.sum(shares.astype(jnp.float32), axis=0).astype(jnp.bfloat16)
+
     owners = image_owner.reshape(n_rep, images)
     requests = image_request.reshape(n_rep, images)
     own_block = lax.dynamic_index_in_dim(owners, me_rep, 0, keepdims=False)
@@ -34,12 +48,15 @@
     earlier = positions[:, None] > positions[None, :]
     rank = jnp.sum((same_owner & earlier).astype(jnp.int32), axis=1, dtype=jnp.int32)
     slot = own_block * slot_cap + rank
-    placing = (jnp.arange(slot_all, dtype=jnp.int32)[:, None] == slot[None, :]).astype(jnp.bfloat16)
-    weight_flat = kv_weight.reshape(block, kvh_all * width2)
-    sq_heads = self_query.shape[1]
-    kvh_local = self_cache.shape[2]
-    group = sq_heads // kvh_local
-    req_count = self_query.shape[0]
+    row_slot = (slot[:, None] * patches + jnp.arange(patches, dtype=jnp.int32)[None, :]).reshape(rows)
+    placing = (
+        jnp.arange(slot_all * patches, dtype=jnp.int32)[:, None] == row_slot[None, :]
+    ).astype(jnp.bfloat16)
+    outgoing = jnp.dot(placing, image_kv, preferred_element_type=jnp.float32).astype(jnp.bfloat16)
+    outgoing = outgoing.reshape(n_rep, slot_cap * patches, width2)
+    arrived = lax.all_to_all(outgoing, "replica", split_axis=0, concat_axis=0, tiled=True)
+    image_kv = arrived.reshape(slot_all * patches, kvh_local, width2)
+
     self_query_rows = self_query.reshape(req_count, kvh_local, group, head_width)
     scores = (
         jnp.einsum(
@@ -74,19 +91,7 @@
     self_out = (
         (numer / total[..., None]).astype(jnp.bfloat16).reshape(req_count, sq_heads, head_width)
     )
-    outgoing = jnp.dot(
-        placing, features.reshape(images, patches * block), preferred_element_type=jnp.float32
-    )
-    outgoing = outgoing.astype(jnp.bfloat16).reshape(n_rep, slot_cap, patches * block)
-    arrived = lax.all_to_all(outgoing, "replica", split_axis=0, concat_axis=0, tiled=True)
-    count = arrived.shape[1]
-    flat = arrived.reshape(n_rep * count * patches, block)
-    product = jnp.dot(flat, weight_flat, preferred_element_type=jnp.float32)
-    partial_value = product.reshape(n_rep, count, patches, kvh_all, width2)
-    summed = lax.psum_scatter(
-        partial_value.astype(jnp.bfloat16), "tensor", scatter_dimension=3, tiled=True
-    )
-    image_kv = summed.reshape(slot_all * patches, kvh_local, width2)
+
     owner_match = (owners == me_rep).astype(jnp.int32)
     rank_all = jnp.cumsum(owner_match, axis=1, dtype=jnp.int32) - owner_match
     slot_ids = jnp.arange(slot_cap, dtype=jnp.int32)
@@ -95,13 +100,8 @@
     )
     slot_live = jnp.sum(chosen, axis=-1, dtype=jnp.int32)
     slot_req = jnp.sum(chosen * requests[:, None, :], axis=-1, dtype=jnp.int32)
-    row_live = (
-        jnp.broadcast_to(slot_live[:, :, None], (n_rep, slot_cap, patches)).reshape(
-            slot_all * patches
-        )
-        > 0
-    )
-    row_req = jnp.broadcast_to(slot_req[:, :, None], (n_rep, slot_cap, patches)).reshape(
+    slot_tag = jnp.where(slot_live > 0, slot_req, -1)
+    row_tag = jnp.broadcast_to(slot_tag[:, :, None], (n_rep, slot_cap, patches)).reshape(
         slot_all * patches
     )
     unscaled_keys = image_kv[..., :head_width].astype(jnp.float32)
@@ -115,7 +115,7 @@
         jnp.einsum("bkgd,skd->bkgs", cquery, image_keys, preferred_element_type=jnp.float32)
         * score_scale
     )
-    mask = row_live[None, :] & (row_req[None, :] == jnp.arange(req_count, dtype=jnp.int32)[:, None])
+    mask = row_tag[None, :] == jnp.arange(req_count, dtype=jnp.int32)[:, None]
     cweight = jnp.where(mask[:, None, None, :], jnp.exp(cscores), jnp.float32(0.0))
     ctotal = jnp.sum(cweight, axis=-1)
     cnumer = jnp.einsum(

time: 156 us -> 71.8 us (0.46)
  the two profiles are of different devices: /device:TPU:6 before, /device:TPU:1 now
where the time goes in v1:
time: 71.8 us; the launch traced here: 71.5 us
  waiting for transfers between devices  38.4 us (53%)
  starting transfers between devices  21.5 us (30%)
  matrix products  7.77 us (11%)
  local copies, waits for them, and re-layouts  1.94 us (3%)
  other arithmetic  1.23 us (2%)
  between operations  0.78 us (1%)
    all_to_all x1, waiting for transfers between devices, local(): lax.all_to_all(partial, 'tensor', split_axis=0, concat_axis=0, tiled=True)  27.3 us
    all_to_all x1, waiting for transfers between devices, local(): lax.all_to_all(outgoing, 'replica', split_axis=0, concat_axis=0, tiled=True)  11 us
    all_to_all x1, starting transfers between devices, local(): lax.all_to_all(partial, 'tensor', split_axis=0, concat_axis=0, tiled=True)  10.9 us
    all_to_all x1, starting transfers between devices, local(): lax.all_to_all(outgoing, 'replica', split_axis=0, concat_axis=0, tiled=True)  10.6 us
    dot_general x1, matrix products, local(): lax.dot_general(flat, kv_weight, (((1,), (0,)), ((), ())), preferred_elem...  4.45 us
  transfers between devices with their start and end apart: 2, of which 2 were waited for; matrix products, arithmetic and copies ran while one was open for 4% of the time, Pallas kernels for 0%

profile of v1, /device:TPU:1, one launch (start us, length us, event | category | flops | bytes accessed | tf_op | source)
XLA Modules:
  0.0 71.5 jit_solution(8068580645486634723)
XLA Ops:
  0.6 1.3 %reshape.229 = bf16[256,960]{1,0:T(8,128)(2,1)S(1)} reshape(bf16[64,4,960]{2,1,0:T(4,128)(2,1)} %param.9) | data formatting | bytes 983040 | tf_op jit(solution)/shard_map/reshape | solution.py:34
  2.0 4.5 %fusion.5 = bf16[8,256,256]{2,1,0:T(8,128)(2,1)} fusion(bf16[960,8,256]{2,1,0:T(8,128)(2,1)} %param.10, bf16[256,960]{1,0:T(8,128)(2,1)S(1)} %reshape.229), kind=kOutput, calls=%fused_computation.3 | convolution fusion | flops 1007157248 | bytes 5472256 | tf_op jit(solution)/shard_map/dot_general | solution.py:35
  6.5 10.9 %all-to-all-start = ((bf16[8,256,256]{2,1,0:T(8,128)(2,1)}), bf16[8,256,256]{2,1,0:T(8,128)(2,1)S(1)}, u32[]{:S(2)}, u32[]{:S(2)}) async-start(bf16[8,256,256]{2,1,0:T(8,128)(2,1)} %fusion.5), calls=%async_computation | async-start | bytes 2097152 | tf_op jit(solution)/shard_map/all_to_all | solution.py:39
  17.4 0.2 convert_reduce_fusion
  17.7 0.1 add.55
  17.8 0.2 reduce_window_sum.11
  18.1 0.1 select_reduce_fusion
  18.3 0.1 copy.19
  18.4 0.1 broadcast_in_dim.51
  18.5 0.1 eq.80
  18.6 0.1 iota_compare_fusion.5
  18.7 0.1 fusion.33
  18.8 0.3 fusion.40
  19.2 27.3 %all-to-all-done = bf16[8,256,256]{2,1,0:T(8,128)(2,1)S(1)} async-done(((bf16[8,256,256]{2,1,0:T(8,128)(2,1)}), bf16[8,256,256]{2,1,0:T(8,128)(2,1)S(1)}, u32[]{:S(2)}, u32[]{:S(2)}) %all-to-all-start) | async-done | bytes 1048608 | tf_op jit(solution)/shard_map/all_to_all | solution.py:39
  46.5 0.1 reduce_sum.69
  46.6 0.9 %fusion.8 = bf16[64,8,256]{2,1,0:T(8,128)(2,1)} fusion(bf16[256,256]{1,0:T(8,128)(2,1)S(1)} %reduce_sum.69, s32[256]{0:T(256)S(1)} %add.55), kind=kOutput, calls=%fused_computation.5 | convolution fusion | flops 67371008 | bytes 394240 | tf_op jit(solution)/shard_map/dot_general | solution.py:55
  47.6 10.6 %all-to-all-start.1 = ((bf16[64,8,256]{2,1,0:T(8,128)(2,1)}), bf16[64,8,256]{2,1,0:T(8,128)(2,1)S(1)}, u32[]{:S(2)}, u32[]{:S(2)}) async-start(bf16[64,8,256]{2,1,0:T(8,128)(2,1)} %fusion.8), calls=%async_computation.1 | async-start | bytes 524288 | tf_op jit(solution)/shard_map/all_to_all | solution.py:57
  58.2 0.1 fusion.38
  58.3 0.8 %fusion.18 = bf16[8,8,128]{2,1,0:T(8,128)(2,1)} fusion(bf16[8,128,1,256]{3,1,0,2:T(8,128)(2,1)S(1)} %bitcast.73, f32[8,8]{1,0:T(8,128)S(1)} %get-tuple-element.5, f32[8,128]{1,0:T(8,128)S(1)} %get-tuple-element.6, f32[8,8]{1,0:T(8,128)S(1)} %get-tuple-element.4, bf16[8,8,128]{2,1,0:T(8,128)(2,1)S(1)} %get-tuple-element.13), kind=kOutput, calls=%fused_computation.19 | convolution fusion | flops 2129920 | bytes 307200 | tf_op jit(solution)/shard_map/bkgs,bskd->bkgd/dot_general | solution.py:82
  59.1 11.0 %all-to-all-done.1 = bf16[64,8,256]{2,1,0:T(8,128)(2,1)S(1)} async-done(((bf16[64,8,256]{2,1,0:T(8,128)(2,1)}), bf16[64,8,256]{2,1,0:T(8,128)(2,1)S(1)}, u32[]{:S(2)}, u32[]{:S(2)}) %all-to-all-start.1) | async-done | bytes 262176 | tf_op jit(solution)/shard_map/all_to_all | solution.py:57
  70.2 0.1 fusion.21
  70.3 0.4 fusion.39
  70.7 0.1 broadcast_select_fusion
  70.8 0.8 %fusion.19 = bf16[8,8,128]{2,1,0:T(8,128)(2,1)} fusion(bf16[512,1,256]{2,0,1:T(8,128)(2,1)S(1)} %bitcast.70, bf16[8,1,8,512]{3,2,0,1:T(8,128)(2,1)S(1)} %get-tuple-element.11, f32[8,8]{1,0:T(8,128)S(1)} %broadcast_select_fusion, pred[8]{0:T(512)(128)(4,1)S(1)} %get-tuple-element.8), kind=kOutput, calls=%fused_computation.20 | convolution fusion | flops 8413184 | bytes 217600 | tf_op jit(solution)/shard_map/bkgs,skd->bkgd/dot_general | solution.py:121
  (25 shorter events, 0.3 us)
Async XLA Ops:
  0.6 69.7 %copy-start = (bf16[8,8,128]{2,1,0:T(8,128)(2,1)S(1)}, bf16[8,8,128]{2,1,0:T(8,128)(2,1)}, u32[]{:S(2)}) copy-start(bf16[8,8,128]{2,1,0:T(8,128)(2,1)} %param.13) | copy-start | bytes 49156
  1.9 15.4 %copy-start.1 = (s32[4096]{0:T(1024)S(1)}, s32[4096]{0:T(1024)}, u32[]{:S(2)}) copy-start(s32[4096]{0:T(1024)} %param.11) | copy-start | bytes 49156
  1.9 16.1 %copy-start.2 = (s32[4096]{0:T(1024)S(1)}, s32[4096]{0:T(1024)}, u32[]{:S(2)}) copy-start(s32[4096]{0:T(1024)} %param.12) | copy-start | bytes 49156
  2.0 16.7 %copy-start.6 = (s32[8]{0:T(128)S(1)}, s32[8]{0:T(128)}, u32[]{:S(2)}) copy-start(s32[8]{0:T(128)} %param.17) | copy-start | bytes 100
  2.0 16.8 %copy-start.3 = (bf16[8,1,256]{2,0,1:T(8,128)(2,1)S(1)}, bf16[8,1,256]{2,0,1:T(8,128)(2,1)}, u32[]{:S(2)}) copy-start(bf16[8,1,256]{2,0,1:T(8,128)(2,1)} %param.16) | copy-start | bytes 12292
  2.0 16.7 %copy-start.5 = (bf16[8,8,128]{2,1,0:T(8,128)(2,1)S(1)}, bf16[8,8,128]{2,1,0:T(8,128)(2,1)}, u32[]{:S(2)}) copy-start(bf16[8,8,128]{2,1,0:T(8,128)(2,1)} %param.14) | copy-start | bytes 49156
  2.0 16.9 %copy-start.4 = (bf16[8,128,1,256]{3,1,2,0:T(8,128)(2,1)S(1)}, bf16[8,128,1,256]{3,1,2,0:T(8,128)(2,1)}, u32[]{:S(2)}) copy-start(bf16[8,128,1,256]{3,1,2,0:T(8,128)(2,1)} %param.15) | copy-start | bytes 1572868
  6.5 40.0 %all-to-all-start = ((bf16[8,256,256]{2,1,0:T(8,128)(2,1)}), bf16[8,256,256]{2,1,0:T(8,128)(2,1)S(1)}, u32[]{:S(2)}, u32[]{:S(2)}) async-start(bf16[8,256,256]{2,1,0:T(8,128)(2,1)} %fusion.5), calls=%async_computation | async-start | bytes 2097152 | tf_op jit(solution)/shard_map/all_to_all | solution.py:39
  47.6 22.6 %all-to-all-start.1 = ((bf16[64,8,256]{2,1,0:T(8,128)(2,1)}), bf16[64,8,256]{2,1,0:T(8,128)(2,1)S(1)}, u32[]{:S(2)}, u32[]{:S(2)}) async-start(bf16[64,8,256]{2,1,0:T(8,128)(2,1)} %fusion.8), calls=%async_computation.1 | async-start | bytes 524288 | tf_op jit(solution)/shard_map/all_to_all | solution.py:57
